TPU v7x, 32 devices: a whole 2x2x4 slice. The times are simulated.
32 devices in a mesh: groups: 2 (over y), cell: 4 (over z), member: 4 (over x, core).
Axes of the slice: x: 2, y: 2, z: 4, core: 2. Of those that a mesh axis runs over, the one named last changes fastest.
Arguments:
- prior_sample_set: float32 [512, 3, 32, 512], P(('groups', 'member'), None, 'cell'), parts along dimension 0, may hold values from -6 to 6
- wind_table: float32 [8, 2], replicated, may hold values from -0.45 to 0.45
- regimes: int32 [16, 4], P('groups'), parts along dimension 0, may hold values from 0 to 7
- obs_index: int32 [8, 512], P(('groups', 'cell')), parts along dimension 0, may hold values from 0 to 4095
- obs_count: int32 [8], P(('groups', 'cell')), parts along dimension 0, may hold values from 1 to 512, as said below
- obs_value: float32 [8, 512], P(('groups', 'cell')), parts along dimension 0, may hold values from -6 to 6
- obs_var: float32 [8, 512], P(('groups', 'cell')), parts along dimension 0, may hold values from 0.25 to 4
Outputs:
- posterior_sample_set: float32 [512, 3, 32, 512], P(('groups', 'member'), None, 'cell'), parts along dimension 0
There are 2 independent parts, one for each index of `groups`. A program takes and returns all parts, laid end to end along the dimension named above; an argument that names none is the same for every part. Nothing has to cross between parts.
Inputs may be any that keep to these rules, and one draw needn't show every extreme that they name: `obs_count`: some tile has exactly 512 live slots.
All inputs are finite; a program needn't handle non-finite values.
Results may differ from a plain program's by a relative error of at most 0.019.
The roundings to bfloat16 on the way count: a program that leaves them out, or rounds other values in their place, can miss the bound.
Values may be sent and summed in bfloat16 or wider, within the bound.
A program may use at most 64 MiB of HBM per device.

v0:
```python
import jax
import jax.numpy as jnp
from jax import lax
from jax.sharding import PartitionSpec as P

SUBSTEPS = 4
BAND = 4
ROOT_STEPS = 24
diffusion = 0.02


def padded_2(cells, sides, width):
    for axis, dim in sides:
        count = lax.axis_size(axis)
        ends = count - 1
        head = lax.slice_in_dim(cells, 0, width, axis=dim)
        tail = lax.slice_in_dim(cells, cells.shape[dim] - width, cells.shape[dim], axis=dim)
        cells = jnp.concatenate(
            [
                lax.ppermute(tail, axis, [(i, (i + 1) % count) for i in range(ends)]),
                cells,
                lax.ppermute(head, axis, [((i + 1) % count, i) for i in range(ends)]),
            ],
            axis=dim,
        )
    return cells


def row_speeds(row_ids, regime_column, wind_table, row_total):
    band_ids = jnp.clip(row_ids, 0, row_total - 1) // BAND
    band_hits = (band_ids[:, None] == jnp.arange(regime_column.shape[0])[None, :]).astype(jnp.int32)
    regime_ids = jnp.sum(band_hits * regime_column[None, :], axis=1)
    regime_hits = (regime_ids[:, None] == jnp.arange(wind_table.shape[0])[None, :]).astype(
        jnp.float32
    )
    speed = jnp.dot(
        regime_hits, wind_table, precision=lax.Precision.HIGHEST, preferred_element_type=jnp.float32
    )
    return (speed[:, 0:1], speed[:, 1:2])


def stencil(padded, speed_x, speed_y):
    centre = padded[..., 1:-1, :]
    south = padded[..., :-2, :]
    north = padded[..., 2:, :]
    widths = [(0, 0)] * (centre.ndim - 1) + [(1, 1)]
    sides = jnp.pad(centre, widths)
    west = sides[..., :-2]
    east = sides[..., 2:]
    result = (
        centre
        - jnp.maximum(speed_x, 0.0) * (centre - south)
        - jnp.minimum(speed_x, 0.0) * (north - centre)
    )
    result = (
        result
        - jnp.maximum(speed_y, 0.0) * (centre - west)
        - jnp.minimum(speed_y, 0.0) * (east - centre)
    )
    return result + diffusion * (north + south + east + west - 4.0 * centre)


def inverse_root(precision_matrix):
    size_n = precision_matrix.shape[0]
    identity = jnp.eye(size_n, dtype=jnp.float32)
    scale = jnp.trace(precision_matrix)
    start = (precision_matrix / scale, identity)

    def newton_step(index, carry):
        upper, lower = carry
        middle = 1.5 * identity - 0.5 * jnp.dot(
            lower, upper, precision=lax.Precision.HIGHEST, preferred_element_type=jnp.float32
        )
        upper = jnp.dot(
            upper, middle, precision=lax.Precision.HIGHEST, preferred_element_type=jnp.float32
        )
        lower = jnp.dot(
            middle, lower, precision=lax.Precision.HIGHEST, preferred_element_type=jnp.float32
        )
        return (upper, lower)

    upper, lower = lax.fori_loop(0, ROOT_STEPS, newton_step, start)
    return (lower, scale)


def analysis(gram, gain, members):
    identity = jnp.eye(members, dtype=jnp.float32)
    precision_matrix = gram + (members - 1.0) * identity
    root_inverse, scale = inverse_root(precision_matrix)
    half_way = jnp.dot(
        root_inverse, gain, precision=lax.Precision.HIGHEST, preferred_element_type=jnp.float32
    )
    mean_weights = (
        jnp.dot(
            root_inverse,
            half_way,
            precision=lax.Precision.HIGHEST,
            preferred_element_type=jnp.float32,
        )
        / scale
    )
    root = jnp.sqrt((members - 1.0) / scale) * root_inverse
    blend = mean_weights[:, None] + root
    transform = blend - jnp.mean(blend, axis=0, keepdims=True) + 1.0 / members
    return transform.astype(jnp.bfloat16)


def observation_terms(predicted, slot_ids, obs_count, obs_value, obs_var):
    ybar = jnp.mean(predicted, axis=0)
    spread = predicted - ybar[None, :]
    live = (slot_ids < obs_count).astype(jnp.float32)
    weight = live / jnp.sqrt(obs_var)
    scaled = spread * weight[None, :]
    gram_part = jnp.dot(
        scaled, scaled.T, precision=lax.Precision.HIGHEST, preferred_element_type=jnp.float32
    )
    innovation = weight * (obs_value - ybar)
    gain_part = jnp.dot(
        scaled, innovation, precision=lax.Precision.HIGHEST, preferred_element_type=jnp.float32
    )
    return (gram_part, gain_part)


def shards(prior_sample_set, wind_table, regimes, obs_index, obs_count, obs_value, obs_var):
    members_on_device = prior_sample_set.shape[0]
    tile_rows = prior_sample_set.shape[2]
    row_total = tile_rows * lax.axis_size("cell")
    first_row = lax.axis_index("cell") * tile_rows
    sample_set_values = prior_sample_set
    for step in range(SUBSTEPS):
        padded = padded_2(sample_set_values, (("cell", 2),), 1)
        row_ids = first_row + jnp.arange(tile_rows)
        speed_x, speed_y = row_speeds(row_ids, regimes[:, step], wind_table, row_total)
        sample_set_values = stencil(padded, speed_x, speed_y)
    first_cloud_cover = sample_set_values[:, 0].reshape(members_on_device, -1)
    slots_total = obs_index.shape[1]
    cell_hits = (jnp.arange(first_cloud_cover.shape[1])[:, None] == obs_index[0][None, :]).astype(
        jnp.float32
    )
    local_pred = jnp.dot(
        first_cloud_cover,
        cell_hits,
        precision=lax.Precision.HIGHEST,
        preferred_element_type=jnp.float32,
    )
    predicted = lax.all_gather(local_pred, "member", axis=0, tiled=True)
    slot_ids = jnp.arange(slots_total)
    gram_part, gain_part = observation_terms(
        predicted, slot_ids, obs_count[0], obs_value[0], obs_var[0]
    )
    gram, gain = lax.psum((gram_part, gain_part), "cell")
    members = gram.shape[0]
    update_matrix_reduced_precise = analysis(gram, gain, members)
    predicted_reduced_precise = sample_set_values.astype(jnp.bfloat16).reshape(
        members_on_device, prior_sample_set.shape[1], -1
    )
    my_columns = lax.dynamic_slice_in_dim(
        update_matrix_reduced_precise,
        lax.axis_index("member") * members_on_device,
        members_on_device,
        1,
    )
    initial = jnp.zeros(predicted_reduced_precise.shape, jnp.float32)
    piece = lax.all_gather(predicted_reduced_precise, "member", axis=0, tiled=True)
    coeffs = lax.slice_in_dim(my_columns, 0, piece.shape[0], axis=0)
    blended = initial + jnp.einsum("ij,ifc->jfc", coeffs, piece, preferred_element_type=jnp.float32)
    return blended.reshape(prior_sample_set.shape)


def solution(mesh):
    return jax.shard_map(
        shards,
        mesh=mesh,
        in_specs=(
            P(("groups", "member"), None, "cell", None),
            P(),
            P("groups", None),
            P(("groups", "cell"), None),
            P(("groups", "cell")),
            P(("groups", "cell"), None),
            P(("groups", "cell"), None),
        ),
        out_specs=P(("groups", "member"), None, "cell", None),
        check_vma=False,
    )
```

profile of v0, /device:TPU:0, one launch (start us, length us, event | category | flops | bytes accessed | tf_op | source)
XLA Modules:
  0.0 187.4 jit_solution(12085723953323743771)
XLA Ops:
  7.4 3.7 %copy.46 = f32[64,3,8,512]{3,0,2,1:T(8,128)S(1)} copy(f32[64,3,8,512]{3,2,1,0:T(8,128)} %param.9) | data formatting | bytes 6291456 | tf_op args[0]
  11.1 0.8 fusion.91
  11.9 5.7 %collective-permute-start = (f32[64,3,1,512]{3,0,2,1:T(8,128)}, f32[64,3,1,512]{3,0,2,1:T(8,128)}, u32[]{:S(2)}, u32[]{:S(2)}) collective-permute-start(f32[64,3,1,512]{3,0,2,1:T(8,128)} %get-tuple-element.68), channel_id=1, source_target_pairs={{0,4},{4,8},{8,12},{1,5},{5,9},{9,13},{2,6},{6,10},{10,14},{3,7},{... | collective-permute-start | bytes 1179656 | tf_op jit(solution)/shard_map/ppermute | solution.py:20
  17.6 1.3 collective-permute-start.1
  18.9 0.6 slice_bitcast_fusion.3
  20.2 0.9 select_reduce_fusion.1
  21.4 4.1 %collective-permute-done = f32[64,3,1,512]{3,0,2,1:T(8,128)} collective-permute-done((f32[64,3,1,512]{3,0,2,1:T(8,128)}, f32[64,3,1,512]{3,0,2,1:T(8,128)}, u32[]{:S(2)}, u32[]{:S(2)}) %collective-permute-start) | collective-permute-done | bytes 393248 | tf_op jit(solution)/shard_map/ppermute | solution.py:20
  25.5 4.6 %collective-permute-done.1 = f32[64,3,1,512]{3,0,2,1:T(8,128)} collective-permute-done((f32[64,3,1,512]{3,0,2,1:T(8,128)S(1)}, f32[64,3,1,512]{3,0,2,1:T(8,128)}, u32[]{:S(2)}, u32[]{:S(2)}) %collective-permute-start.1) | collective-permute-done | bytes 393248 | tf_op jit(solution)/shard_map/ppermute | solution.py:22
  30.2 4.2 %fusion.53 = f32[64,3,8,512]{3,0,2,1:T(8,128)S(1)} fusion(f32[64,3,1,512]{3,0,2,1:T(8,128)} %collective-permute-done.1, f32[64,3,8,512]{3,0,2,1:T(8,128)S(1)} %copy.46, f32[64,3,1,512]{3,0,2,1:T(8,128)} %collective-permute-done, f32[8]{0:T(128)S(1)} %get-tuple-element.92, f32[8]{0:T(128)S(1)} %get-tuple-element.93, f32[8]{0:T(128)S(1)} %get-tuple-element.91, ...), kind=kLoop, calls=%fused_computation.71 | loop fusion | flops 16515072 | bytes 7078016 | tf_op jit(solution)/shard_map/add | solution.py:60
  34.5 2.8 %collective-permute-start.2 = (f32[64,3,1,512]{3,0,2,1:T(8,128)S(1)}, f32[64,3,1,512]{3,0,2,1:T(8,128)S(1)}, u32[]{:S(2)}, u32[]{:S(2)}) collective-permute-start(f32[64,3,1,512]{3,0,2,1:T(8,128)S(1)} %get-tuple-element.66), channel_id=1, source_target_pairs={{0,4},{4,8},{8,12},{1,5},{5,9},{9,13},{2,6},{6,10},{10,14},{3,7},{... | collective-permute-start | bytes 1179656 | tf_op jit(solution)/shard_map/ppermute | solution.py:20
  37.2 1.3 collective-permute-start.3
  38.7 5.7 %collective-permute-done.2 = f32[64,3,1,512]{3,0,2,1:T(8,128)S(1)} collective-permute-done((f32[64,3,1,512]{3,0,2,1:T(8,128)S(1)}, f32[64,3,1,512]{3,0,2,1:T(8,128)S(1)}, u32[]{:S(2)}, u32[]{:S(2)}) %collective-permute-start.2) | collective-permute-done | bytes 393248 | tf_op jit(solution)/shard_map/ppermute | solution.py:20
  44.4 4.1 %collective-permute-done.3 = f32[64,3,1,512]{3,0,2,1:T(8,128)S(1)} collective-permute-done((f32[64,3,1,512]{3,0,2,1:T(8,128)S(1)}, f32[64,3,1,512]{3,0,2,1:T(8,128)S(1)}, u32[]{:S(2)}, u32[]{:S(2)}) %collective-permute-start.3) | collective-permute-done | bytes 393248 | tf_op jit(solution)/shard_map/ppermute | solution.py:22
  48.5 3.1 %fusion.39 = f32[64,3,8,512]{3,0,2,1:T(8,128)S(1)} fusion(f32[64,3,1,512]{3,0,2,1:T(8,128)S(1)} %collective-permute-done.3, f32[64,3,8,512]{3,0,2,1:T(8,128)S(1)} %fusion.53, f32[64,3,1,512]{3,0,2,1:T(8,128)S(1)} %collective-permute-done.2, f32[8]{0:T(128)S(1)} %get-tuple-element.88, f32[8]{0:T(128)S(1)} %get-tuple-element.89, f32[8]{0:T(128)S(1)} %get-tuple-element.87, ...), kind=kLoop, calls=%fused_computation.55 | loop fusion | flops 16515072 | bytes 7078016 | tf_op jit(solution)/shard_map/add | solution.py:60
  51.7 3.5 %collective-permute-start.4 = (f32[64,3,1,512]{3,0,2,1:T(8,128)S(1)}, f32[64,3,1,512]{3,0,2,1:T(8,128)S(1)}, u32[]{:S(2)}, u32[]{:S(2)}) collective-permute-start(f32[64,3,1,512]{3,0,2,1:T(8,128)S(1)} %get-tuple-element.64), channel_id=1, source_target_pairs={{0,4},{4,8},{8,12},{1,5},{5,9},{9,13},{2,6},{6,10},{10,14},{3,7},{... | collective-permute-start | bytes 1179656 | tf_op jit(solution)/shard_map/ppermute | solution.py:20
  55.2 1.3 collective-permute-start.5
  56.7 4.4 %collective-permute-done.4 = f32[64,3,1,512]{3,0,2,1:T(8,128)S(1)} collective-permute-done((f32[64,3,1,512]{3,0,2,1:T(8,128)S(1)}, f32[64,3,1,512]{3,0,2,1:T(8,128)S(1)}, u32[]{:S(2)}, u32[]{:S(2)}) %collective-permute-start.4) | collective-permute-done | bytes 393248 | tf_op jit(solution)/shard_map/ppermute | solution.py:20
  61.1 4.1 %collective-permute-done.5 = f32[64,3,1,512]{3,0,2,1:T(8,128)S(1)} collective-permute-done((f32[64,3,1,512]{3,0,2,1:T(8,128)S(1)}, f32[64,3,1,512]{3,0,2,1:T(8,128)S(1)}, u32[]{:S(2)}, u32[]{:S(2)}) %collective-permute-start.5) | collective-permute-done | bytes 393248 | tf_op jit(solution)/shard_map/ppermute | solution.py:22
  65.3 3.2 %fusion.25 = f32[64,3,8,512]{3,0,2,1:T(8,128)S(1)} fusion(f32[64,3,1,512]{3,0,2,1:T(8,128)S(1)} %collective-permute-done.5, f32[64,3,8,512]{3,0,2,1:T(8,128)S(1)} %fusion.39, f32[64,3,1,512]{3,0,2,1:T(8,128)S(1)} %collective-permute-done.4, f32[8]{0:T(128)S(1)} %get-tuple-element.84, f32[8]{0:T(128)S(1)} %get-tuple-element.85, f32[8]{0:T(128)S(1)} %get-tuple-element.83, ...), kind=kLoop, calls=%fused_computation.39 | loop fusion | flops 16515072 | bytes 7078016 | tf_op jit(solution)/shard_map/add | solution.py:60
  68.5 2.5 %collective-permute-start.6 = (f32[64,3,1,512]{3,0,2,1:T(8,128)S(1)}, f32[64,3,1,512]{3,0,2,1:T(8,128)S(1)}, u32[]{:S(2)}, u32[]{:S(2)}) collective-permute-start(f32[64,3,1,512]{3,0,2,1:T(8,128)S(1)} %get-tuple-element.62), channel_id=1, source_target_pairs={{0,4},{4,8},{8,12},{1,5},{5,9},{9,13},{2,6},{6,10},{10,14},{3,7},{... | collective-permute-start | bytes 1179656 | tf_op jit(solution)/shard_map/ppermute | solution.py:20
  71.0 1.3 collective-permute-start.7
  72.4 3.9 %collective-permute-done.6 = f32[64,3,1,512]{3,0,2,1:T(8,128)S(1)} collective-permute-done((f32[64,3,1,512]{3,0,2,1:T(8,128)S(1)}, f32[64,3,1,512]{3,0,2,1:T(8,128)S(1)}, u32[]{:S(2)}, u32[]{:S(2)}) %collective-permute-start.6) | collective-permute-done | bytes 393248 | tf_op jit(solution)/shard_map/ppermute | solution.py:20
  76.3 4.4 %collective-permute-done.7 = f32[64,3,1,512]{3,0,2,1:T(8,128)S(1)} collective-permute-done((f32[64,3,1,512]{3,0,2,1:T(8,128)S(1)}, f32[64,3,1,512]{3,0,2,1:T(8,128)S(1)}, u32[]{:S(2)}, u32[]{:S(2)}) %collective-permute-start.7) | collective-permute-done | bytes 393248 | tf_op jit(solution)/shard_map/ppermute | solution.py:22
  80.7 3.4 %convert_bitcast_fusion = (bf16[3,8,8,8,512]{4,3,2,1,0:T(8,128)(2,1)S(1)}, f32[64,3,8,512]{3,0,2,1:T(8,128)S(1)}) fusion(f32[64,3,8,512]{3,0,2,1:T(8,128)S(1)} %fusion.25, f32[8]{0:T(128)S(1)} %get-tuple-element.80, f32[8]{0:T(128)S(1)} %get-tuple-element.81, f32[64,3,1,512]{3,0,2,1:T(8,128)S(1)} %collective-permute-done.7, f32[8]{0:T(128)S(1)} %get-tuple-element.79, ...), kind=kLoop, calls=%fused_computation.80 | loop fusion | flops 17301504 | bytes 8650880
  84.2 0.5 copy-done.4
  84.7 3.0 %fusion.3 = f32[64,512]{1,0:T(8,128)S(1)} fusion(f32[64,4096]{1,0:T(8,128)S(1)} %bitcast.108, s32[512]{0:T(512)S(1)} %bitcast.117), kind=kOutput, calls=%fused_computation.6 | convolution fusion | flops 1612709888 | bytes 1181696 | tf_op jit(solution)/shard_map/dot_general | solution.py:140
  87.8 7.4 %all_gather.6 = f32[256,512]{1,0:T(8,128)S(1)} all-gather(f32[64,512]{1,0:T(8,128)S(1)} %fusion.3), channel_id=1, replica_groups=mesh['groups'=2,'cell'=4,'member'=4] {'member'}, dimensions={0}, use_global_device_ids=true | all-gather | bytes 655360 | tf_op jit(solution)/shard_map/all_gather | solution.py:146
  95.2 1.4 fusion.62
  96.7 1.3 copy.59
  98.0 0.5 fusion.61
  98.5 8.6 %psum.15 = f32[256]{0:T(256)S(1)} all-reduce(f32[256]{0:T(256)S(1)} %bitcast.114), channel_id=1, replica_groups=mesh['groups'=2,'cell'=4,'member'=4] {'cell'}, use_global_device_ids=true, to_apply=%region_9.10 | all-reduce | flops 256 | bytes 2048 | tf_op jit(solution)/shard_map/psum | solution.py:151
  107.2 22.7 %all-reduce.6.cloned.1.call-done = f32[256,256]{1,0:T(8,128)} async-done(((f32[256,256]{1,0:T(8,128)}), f32[256,256]{1,0:T(8,128)}) %all-reduce.6.cloned.1.call-update) | async-done | bytes 262160 | tf_op jit(solution)/shard_map/psum | solution.py:151
  129.9 1.7 select_reduce_fusion
  131.6 1.7 fusion.68
  133.4 35.4 %while.13 = (s32[]{:T(128)}, f32[256,256]{0,1:T(8,128)S(1)}, f32[256,256]{1,0:T(8,128)S(1)}, s32[]{:T(128)}) while((s32[]{:T(128)}, f32[256,256]{0,1:T(8,128)S(1)}, f32[256,256]{1,0:T(8,128)S(1)}, s32[]{:T(128)}) %tuple.51), condition=%wide.region_8.9_spmd.clone, body=%wide.region_7.8_spmd.clone.sunk | while | flops 604241920 | bytes 3407925 | solution.py:82
  133.4 0.4 fusion.126
  134.2 0.6 convolution_bitcast_fusion.3
  135.7 0.6 convolution_bitcast_fusion.3
  137.2 0.6 convolution_bitcast_fusion.3
  138.7 0.6 convolution_bitcast_fusion.3
  140.1 0.6 convolution_bitcast_fusion.3
  141.6 0.6 convolution_bitcast_fusion.3
  143.1 0.6 convolution_bitcast_fusion.3
  144.6 0.6 convolution_bitcast_fusion.3
  146.0 0.6 convolution_bitcast_fusion.3
  147.5 0.6 convolution_bitcast_fusion.3
  149.0 0.6 convolution_bitcast_fusion.3
  150.4 0.6 convolution_bitcast_fusion.3
  151.9 0.6 convolution_bitcast_fusion.3
  153.4 0.6 convolution_bitcast_fusion.3
  154.9 0.6 convolution_bitcast_fusion.3
  156.3 0.6 convolution_bitcast_fusion.3
  157.8 0.6 convolution_bitcast_fusion.3
  159.3 0.6 convolution_bitcast_fusion.3
  160.8 0.6 convolution_bitcast_fusion.3
  162.2 0.6 convolution_bitcast_fusion.3
  163.7 0.6 convolution_bitcast_fusion.3
  165.2 0.6 convolution_bitcast_fusion.3
  166.7 0.6 convolution_bitcast_fusion.3
  168.1 0.6 convolution_bitcast_fusion.3
  170.3 0.7 broadcast_divide_fusion
  171.2 4.0 %fusion.72 = f32[64,3,4096]{2,0,1:T(8,128)S(1)} fusion(bf16[256,3,4096]{2,0,1:T(8,128)(2,1)} %all-gather.2.cloned.1.call-done, f32[256,256]{0,1:T(8,128)S(1)} %get-tuple-element.59, s32[]{:T(128)S(6)} %select_n.22, f32[64]{0:T(128)S(1)} %dynamic-slice), kind=kOutput, calls=%fused_computation.99 | convolution fusion | flops 402702336 | bytes 9503236 | tf_op jit(solution)/shard_map/ij,ifc->jfc/dot_general | solution.py:166
  175.3 2.7 %copy.61 = f32[24,8,8,512]{3,2,1,0:T(8,128)S(1)} copy(f32[24,8,8,512]{3,1,2,0:T(8,128)S(1)} %bitcast.105) | data formatting | bytes 6291456
  178.0 2.0 %copy.58 = f32[64,3,8,512]{3,2,1,0:T(8,128)} copy(f32[64,3,8,512]{3,2,0,1:T(8,128)S(1)} %bitcast.106) | data formatting | bytes 6291456 | tf_op jit(solution)/shard_map/reshape | solution.py:167
  (134 shorter events, 21.7 us)
Async XLA Ops:
  7.4 13.7 %copy-start = (f32[8,2]{0,1:T(2,128)S(1)}, f32[8,2]{0,1:T(2,128)}, u32[]{:S(2)}) copy-start(f32[8,2]{0,1:T(2,128)} %param.10) | copy-start | bytes 196
  7.4 11.5 %copy-start.1 = (s32[8,4]{0,1:T(4,128)S(1)}, s32[8,4]{0,1:T(4,128)}, u32[]{:S(2)}) copy-start(s32[8,4]{0,1:T(4,128)} %param.11) | copy-start | bytes 388
  7.4 122.5 %all-reduce.6.cloned.1.call-start = ((), (), s32[]{:S(2)}) async-start(), calls=%async_computation | async-start | bytes 524288 | tf_op jit(solution)/shard_map/psum | solution.py:151
  11.9 13.6 %collective-permute-start = (f32[64,3,1,512]{3,0,2,1:T(8,128)}, f32[64,3,1,512]{3,0,2,1:T(8,128)}, u32[]{:S(2)}, u32[]{:S(2)}) collective-permute-start(f32[64,3,1,512]{3,0,2,1:T(8,128)} %get-tuple-element.68), channel_id=1, source_target_pairs={{0,4},{4,8},{8,12},{1,5},{5,9},{9,13},{2,6},{6,10},{10,14},{3,7},{... | collective-permute-start | bytes 1179656 | tf_op jit(solution)/shard_map/ppermute | solution.py:20
  17.6 12.6 %collective-permute-start.1 = (f32[64,3,1,512]{3,0,2,1:T(8,128)S(1)}, f32[64,3,1,512]{3,0,2,1:T(8,128)}, u32[]{:S(2)}, u32[]{:S(2)}) collective-permute-start(f32[64,3,1,512]{3,0,2,1:T(8,128)S(1)} %get-tuple-element.69), channel_id=1, source_target_pairs={{4,0},{8,4},{12,8},{5,1},{9,5},{13,9},{6,2},{10,6},{14,10},{7,3},{... | collective-permute-start | bytes 1179656 | tf_op jit(solution)/shard_map/ppermute | solution.py:22
  34.5 9.9 %collective-permute-start.2 = (f32[64,3,1,512]{3,0,2,1:T(8,128)S(1)}, f32[64,3,1,512]{3,0,2,1:T(8,128)S(1)}, u32[]{:S(2)}, u32[]{:S(2)}) collective-permute-start(f32[64,3,1,512]{3,0,2,1:T(8,128)S(1)} %get-tuple-element.66), channel_id=1, source_target_pairs={{0,4},{4,8},{8,12},{1,5},{5,9},{9,13},{2,6},{6,10},{10,14},{3,7},{... | collective-permute-start | bytes 1179656 | tf_op jit(solution)/shard_map/ppermute | solution.py:20
  37.2 11.3 %collective-permute-start.3 = (f32[64,3,1,512]{3,0,2,1:T(8,128)S(1)}, f32[64,3,1,512]{3,0,2,1:T(8,128)S(1)}, u32[]{:S(2)}, u32[]{:S(2)}) collective-permute-start(f32[64,3,1,512]{3,0,2,1:T(8,128)S(1)} %get-tuple-element.67), channel_id=1, source_target_pairs={{4,0},{8,4},{12,8},{5,1},{9,5},{13,9},{6,2},{10,6},{14,10},{7,3},{... | collective-permute-start | bytes 1179656 | tf_op jit(solution)/shard_map/ppermute | solution.py:22
  51.7 9.4 %collective-permute-start.4 = (f32[64,3,1,512]{3,0,2,1:T(8,128)S(1)}, f32[64,3,1,512]{3,0,2,1:T(8,128)S(1)}, u32[]{:S(2)}, u32[]{:S(2)}) collective-permute-start(f32[64,3,1,512]{3,0,2,1:T(8,128)S(1)} %get-tuple-element.64), channel_id=1, source_target_pairs={{0,4},{4,8},{8,12},{1,5},{5,9},{9,13},{2,6},{6,10},{10,14},{3,7},{... | collective-permute-start | bytes 1179656 | tf_op jit(solution)/shard_map/ppermute | solution.py:20
  55.2 10.1 %collective-permute-start.5 = (f32[64,3,1,512]{3,0,2,1:T(8,128)S(1)}, f32[64,3,1,512]{3,0,2,1:T(8,128)S(1)}, u32[]{:S(2)}, u32[]{:S(2)}) collective-permute-start(f32[64,3,1,512]{3,0,2,1:T(8,128)S(1)} %get-tuple-element.65), channel_id=1, source_target_pairs={{4,0},{8,4},{12,8},{5,1},{9,5},{13,9},{6,2},{10,6},{14,10},{7,3},{... | collective-permute-start | bytes 1179656 | tf_op jit(solution)/shard_map/ppermute | solution.py:22
  65.3 7.1 %copy-start.2 = (f32[1,512]{1,0:T(1,128)S(1)}, f32[1,512]{1,0:T(1,128)}, u32[]{:S(2)}) copy-start(f32[1,512]{1,0:T(1,128)} %param.15) | copy-start | bytes 6148
  68.5 7.7 %collective-permute-start.6 = (f32[64,3,1,512]{3,0,2,1:T(8,128)S(1)}, f32[64,3,1,512]{3,0,2,1:T(8,128)S(1)}, u32[]{:S(2)}, u32[]{:S(2)}) collective-permute-start(f32[64,3,1,512]{3,0,2,1:T(8,128)S(1)} %get-tuple-element.62), channel_id=1, source_target_pairs={{0,4},{4,8},{8,12},{1,5},{5,9},{9,13},{2,6},{6,10},{10,14},{3,7},{... | collective-permute-start | bytes 1179656 | tf_op jit(solution)/shard_map/ppermute | solution.py:20
  71.0 9.7 %collective-permute-start.7 = (f32[64,3,1,512]{3,0,2,1:T(8,128)S(1)}, f32[64,3,1,512]{3,0,2,1:T(8,128)S(1)}, u32[]{:S(2)}, u32[]{:S(2)}) collective-permute-start(f32[64,3,1,512]{3,0,2,1:T(8,128)S(1)} %get-tuple-element.63), channel_id=1, source_target_pairs={{4,0},{8,4},{12,8},{5,1},{9,5},{13,9},{6,2},{10,6},{14,10},{7,3},{... | collective-permute-start | bytes 1179656 | tf_op jit(solution)/shard_map/ppermute | solution.py:22
  84.1 0.7 copy-start.4
  84.1 11.1 %copy-start.3 = (f32[1,512]{1,0:T(1,128)S(1)}, f32[1,512]{1,0:T(1,128)}, u32[]{:S(2)}) copy-start(f32[1,512]{1,0:T(1,128)} %param.14) | copy-start | bytes 6148
  96.6 74.6 %all-gather.2.cloned.1.call-start = ((), (), s32[]{:S(2)}) async-start(), calls=%async_computation.1 | async-start | bytes 7864320 | tf_op jit(solution)/shard_map/all_gather | solution.py:164
Sparse Core Ops, SparseCore 0:
  96.7 33.1 all-reduce.5
Sparse Core Ops, SparseCore 1:
  107.3 44.9 all-gather.1
where the time goes:
time: 188 us; the launch traced here: 187 us
  waiting for transfers between devices  58.2 us (31%)
  matrix products  43.5 us (23%)
  starting transfers between devices  19.6 us (10%)
  other arithmetic  19.1 us (10%)
  between operations  16.5 us (9%)
  blocking collectives  16 us (9%)
  local copies, waits for them, and re-layouts  13.2 us (7%)
    psum x1, waiting for transfers between devices, shards(): gram, gain = lax.psum((gram_part, gain_part), 'cell')  22.7 us
    ppermute x4, waiting for transfers between devices, padded_2(): lax.ppermute(tail, axis, [(i, (i + 1) % count) for i in range(ends)])  18.1 us
    ppermute x4, waiting for transfers between devices, padded_2(): lax.ppermute(head, axis, [((i + 1) % count, i) for i in range(ends)])  17.3 us
    ppermute x4, starting transfers between devices, padded_2(): lax.ppermute(tail, axis, [(i, (i + 1) % count) for i in range(ends)])  14.4 us
    dot_general x24, matrix products, newton_step(): jnp.dot(upper, middle, precision=lax.Precision.HIGHEST, preferred_element...  14.3 us
    add x3, other arithmetic, stencil(): return result + diffusion * (north + south + east + west - 4.0 * centre)  10.5 us
    dot_general x24, matrix products, newton_step(): jnp.dot(lower, upper, precision=lax.Precision.HIGHEST, preferred_element_...  9.83 us
    dot_general x24, matrix products, newton_step(): jnp.dot(middle, lower, precision=lax.Precision.HIGHEST, preferred_element...  9.07 us
  transfers between devices with their start and end apart: 10, of which 9 were waited for; matrix products, arithmetic and copies ran while one was open for 23% of the time, Pallas kernels for 0%

commit v1 on v0

--- a/solution.py
+++ b/solution.py
@@ -122,6 +122,22 @@
 
 
 def shards(prior_sample_set, wind_table, regimes, obs_index, obs_count, obs_value, obs_var):
+
+    def refer_stops_all(dim_k, view):
+        heap = [view]
+        nd = lax.psum(1, "member")
+        for tick in tuple(range(nd - 1)):
+            heap.append(
+                lax.ppermute(
+                    heap[-1], axis_name="member", perm=[(u, (u + 1) % nd) for u in range(nd)]
+                )
+            )
+        return jnp.roll(
+            jnp.concatenate(heap[::-1], dim_k),
+            (lax.axis_index("member") + 1) * view.shape[dim_k],
+            axis=dim_k,
+        )
+
     members_on_device = prior_sample_set.shape[0]
     tile_rows = prior_sample_set.shape[2]
     row_total = tile_rows * lax.axis_size("cell")
@@ -143,7 +159,7 @@
         precision=lax.Precision.HIGHEST,
         preferred_element_type=jnp.float32,
     )
-    predicted = lax.all_gather(local_pred, "member", axis=0, tiled=True)
+    predicted = refer_stops_all(0, local_pred)
     slot_ids = jnp.arange(slots_total)
     gram_part, gain_part = observation_terms(
         predicted, slot_ids, obs_count[0], obs_value[0], obs_var[0]

time: 188 us -> 194 us (1.032)
  waiting for transfers between devices: 58.2 us -> 71.8 us
  blocking collectives: 16 us -> 8.65 us
    ppermute x0 -> x3, waiting for transfers between devices: none -> 12.5 us  [refer_stops_all(): lax.ppermute(heap[-1], axis_name='member', perm=[(u, (u + 1) % nd) for u...]
    all_gather x1 -> x0, blocking collectives: 7.35 us -> none  [shards(): predicted = lax.all_gather(local_pred, 'member', axis=0, tiled=True)]
    unnamed x15 -> x22, local copies, waits for them, and re-layouts: 7.25 us -> 7.32 us
  transfers between devices with their start and end apart: 10 -> 13, of which waited for: 9 -> 12; matrix products, arithmetic and copies ran while one was open for 23% -> 22% of each run, Pallas kernels for 0% -> 0%
where the time goes in v1:
time: 194 us
  waiting for transfers between devices  71.8 us (37%)
  matrix products  43.5 us (22%)
  starting transfers between devices  19.7 us (10%)
  other arithmetic  19.1 us (10%)
  between operations  16.6 us (9%)
  local copies, waits for them, and re-layouts  13.3 us (7%)
  blocking collectives  8.65 us (4%)
    psum x1, waiting for transfers between devices, shards(): gram, gain = lax.psum((gram_part, gain_part), 'cell')  23.2 us
    ppermute x4, waiting for transfers between devices, padded_2(): lax.ppermute(tail, axis, [(i, (i + 1) % count) for i in range(ends)])  18.8 us
    ppermute x4, waiting for transfers between devices, padded_2(): lax.ppermute(head, axis, [((i + 1) % count, i) for i in range(ends)])  17.3 us
    ppermute x4, starting transfers between devices, padded_2(): lax.ppermute(tail, axis, [(i, (i + 1) % count) for i in range(ends)])  14.4 us
    dot_general x24, matrix products, newton_step(): jnp.dot(upper, middle, precision=lax.Precision.HIGHEST, preferred_element...  14.3 us
    ppermute x3, waiting for transfers between devices, refer_stops_all(): lax.ppermute(heap[-1], axis_name='member', perm=[(u, (u + 1) % nd) for u...  12.5 us
    add x3, other arithmetic, stencil(): return result + diffusion * (north + south + east + west - 4.0 * centre)  10.5 us
    dot_general x24, matrix products, newton_step(): jnp.dot(lower, upper, precision=lax.Precision.HIGHEST, preferred_element_...  9.83 us
  transfers between devices with their start and end apart: 13, of which 12 were waited for; matrix products, arithmetic and copies ran while one was open for 22% of the time, Pallas kernels for 0%

profile of v1, /device:TPU:0, one launch (start us, length us, event | category | flops | bytes accessed | tf_op | source)
XLA Modules:
  0.0 194.0 jit_solution(14428742364471341344)
XLA Ops:
  7.4 3.7 %copy.46 = f32[64,3,8,512]{3,0,2,1:T(8,128)S(1)} copy(f32[64,3,8,512]{3,2,1,0:T(8,128)} %param.9) | data formatting | bytes 6291456 | tf_op args[0]
  11.1 0.8 fusion.93
  11.9 5.7 %collective-permute-start = (f32[64,3,1,512]{3,0,2,1:T(8,128)}, f32[64,3,1,512]{3,0,2,1:T(8,128)}, u32[]{:S(2)}, u32[]{:S(2)}) collective-permute-start(f32[64,3,1,512]{3,0,2,1:T(8,128)} %get-tuple-element.68), channel_id=1, source_target_pairs={{0,4},{4,8},{8,12},{1,5},{5,9},{9,13},{2,6},{6,10},{10,14},{3,7},{... | collective-permute-start | bytes 1179656 | tf_op jit(solution)/shard_map/ppermute | solution.py:20
  17.6 1.3 collective-permute-start.1
  18.9 0.6 slice_bitcast_fusion.3
  19.5 0.9 select_reduce_fusion.1
  20.6 4.9 %collective-permute-done = f32[64,3,1,512]{3,0,2,1:T(8,128)} collective-permute-done((f32[64,3,1,512]{3,0,2,1:T(8,128)}, f32[64,3,1,512]{3,0,2,1:T(8,128)}, u32[]{:S(2)}, u32[]{:S(2)}) %collective-permute-start) | collective-permute-done | bytes 393248 | tf_op jit(solution)/shard_map/ppermute | solution.py:20
  25.5 4.6 %collective-permute-done.1 = f32[64,3,1,512]{3,0,2,1:T(8,128)} collective-permute-done((f32[64,3,1,512]{3,0,2,1:T(8,128)S(1)}, f32[64,3,1,512]{3,0,2,1:T(8,128)}, u32[]{:S(2)}, u32[]{:S(2)}) %collective-permute-start.1) | collective-permute-done | bytes 393248 | tf_op jit(solution)/shard_map/ppermute | solution.py:22
  30.2 4.2 %fusion.53 = f32[64,3,8,512]{3,0,2,1:T(8,128)S(1)} fusion(f32[64,3,1,512]{3,0,2,1:T(8,128)} %collective-permute-done.1, f32[64,3,8,512]{3,0,2,1:T(8,128)S(1)} %copy.46, f32[64,3,1,512]{3,0,2,1:T(8,128)} %collective-permute-done, f32[8]{0:T(128)S(1)} %get-tuple-element.92, f32[8]{0:T(128)S(1)} %get-tuple-element.93, f32[8]{0:T(128)S(1)} %get-tuple-element.91, ...), kind=kLoop, calls=%fused_computation.71 | loop fusion | flops 16515072 | bytes 7078016 | tf_op jit(solution)/shard_map/add | solution.py:60
  34.4 2.8 %collective-permute-start.2 = (f32[64,3,1,512]{3,0,2,1:T(8,128)S(1)}, f32[64,3,1,512]{3,0,2,1:T(8,128)S(1)}, u32[]{:S(2)}, u32[]{:S(2)}) collective-permute-start(f32[64,3,1,512]{3,0,2,1:T(8,128)S(1)} %get-tuple-element.66), channel_id=1, source_target_pairs={{0,4},{4,8},{8,12},{1,5},{5,9},{9,13},{2,6},{6,10},{10,14},{3,7},{... | collective-permute-start | bytes 1179656 | tf_op jit(solution)/shard_map/ppermute | solution.py:20
  37.2 1.3 collective-permute-start.3
  38.7 5.6 %collective-permute-done.2 = f32[64,3,1,512]{3,0,2,1:T(8,128)S(1)} collective-permute-done((f32[64,3,1,512]{3,0,2,1:T(8,128)S(1)}, f32[64,3,1,512]{3,0,2,1:T(8,128)S(1)}, u32[]{:S(2)}, u32[]{:S(2)}) %collective-permute-start.2) | collective-permute-done | bytes 393248 | tf_op jit(solution)/shard_map/ppermute | solution.py:20
  44.4 4.1 %collective-permute-done.3 = f32[64,3,1,512]{3,0,2,1:T(8,128)S(1)} collective-permute-done((f32[64,3,1,512]{3,0,2,1:T(8,128)S(1)}, f32[64,3,1,512]{3,0,2,1:T(8,128)S(1)}, u32[]{:S(2)}, u32[]{:S(2)}) %collective-permute-start.3) | collective-permute-done | bytes 393248 | tf_op jit(solution)/shard_map/ppermute | solution.py:22
  48.5 3.1 %fusion.39 = f32[64,3,8,512]{3,0,2,1:T(8,128)S(1)} fusion(f32[64,3,1,512]{3,0,2,1:T(8,128)S(1)} %collective-permute-done.3, f32[64,3,8,512]{3,0,2,1:T(8,128)S(1)} %fusion.53, f32[64,3,1,512]{3,0,2,1:T(8,128)S(1)} %collective-permute-done.2, f32[8]{0:T(128)S(1)} %get-tuple-element.88, f32[8]{0:T(128)S(1)} %get-tuple-element.89, f32[8]{0:T(128)S(1)} %get-tuple-element.87, ...), kind=kLoop, calls=%fused_computation.55 | loop fusion | flops 16515072 | bytes 7078016 | tf_op jit(solution)/shard_map/add | solution.py:60
  51.7 3.5 %collective-permute-start.4 = (f32[64,3,1,512]{3,0,2,1:T(8,128)S(1)}, f32[64,3,1,512]{3,0,2,1:T(8,128)S(1)}, u32[]{:S(2)}, u32[]{:S(2)}) collective-permute-start(f32[64,3,1,512]{3,0,2,1:T(8,128)S(1)} %get-tuple-element.64), channel_id=1, source_target_pairs={{0,4},{4,8},{8,12},{1,5},{5,9},{9,13},{2,6},{6,10},{10,14},{3,7},{... | collective-permute-start | bytes 1179656 | tf_op jit(solution)/shard_map/ppermute | solution.py:20
  55.2 1.3 collective-permute-start.5
  56.7 4.4 %collective-permute-done.4 = f32[64,3,1,512]{3,0,2,1:T(8,128)S(1)} collective-permute-done((f32[64,3,1,512]{3,0,2,1:T(8,128)S(1)}, f32[64,3,1,512]{3,0,2,1:T(8,128)S(1)}, u32[]{:S(2)}, u32[]{:S(2)}) %collective-permute-start.4) | collective-permute-done | bytes 393248 | tf_op jit(solution)/shard_map/ppermute | solution.py:20
  61.1 4.1 %collective-permute-done.5 = f32[64,3,1,512]{3,0,2,1:T(8,128)S(1)} collective-permute-done((f32[64,3,1,512]{3,0,2,1:T(8,128)S(1)}, f32[64,3,1,512]{3,0,2,1:T(8,128)S(1)}, u32[]{:S(2)}, u32[]{:S(2)}) %collective-permute-start.5) | collective-permute-done | bytes 393248 | tf_op jit(solution)/shard_map/ppermute | solution.py:22
  65.3 3.2 %fusion.25 = f32[64,3,8,512]{3,0,2,1:T(8,128)S(1)} fusion(f32[64,3,1,512]{3,0,2,1:T(8,128)S(1)} %collective-permute-done.5, f32[64,3,8,512]{3,0,2,1:T(8,128)S(1)} %fusion.39, f32[64,3,1,512]{3,0,2,1:T(8,128)S(1)} %collective-permute-done.4, f32[8]{0:T(128)S(1)} %get-tuple-element.84, f32[8]{0:T(128)S(1)} %get-tuple-element.85, f32[8]{0:T(128)S(1)} %get-tuple-element.83, ...), kind=kLoop, calls=%fused_computation.39 | loop fusion | flops 16515072 | bytes 7078016 | tf_op jit(solution)/shard_map/add | solution.py:60
  68.5 2.5 %collective-permute-start.6 = (f32[64,3,1,512]{3,0,2,1:T(8,128)S(1)}, f32[64,3,1,512]{3,0,2,1:T(8,128)S(1)}, u32[]{:S(2)}, u32[]{:S(2)}) collective-permute-start(f32[64,3,1,512]{3,0,2,1:T(8,128)S(1)} %get-tuple-element.62), channel_id=1, source_target_pairs={{0,4},{4,8},{8,12},{1,5},{5,9},{9,13},{2,6},{6,10},{10,14},{3,7},{... | collective-permute-start | bytes 1179656 | tf_op jit(solution)/shard_map/ppermute | solution.py:20
  71.0 1.3 collective-permute-start.7
  72.5 3.8 %collective-permute-done.6 = f32[64,3,1,512]{3,0,2,1:T(8,128)S(1)} collective-permute-done((f32[64,3,1,512]{3,0,2,1:T(8,128)S(1)}, f32[64,3,1,512]{3,0,2,1:T(8,128)S(1)}, u32[]{:S(2)}, u32[]{:S(2)}) %collective-permute-start.6) | collective-permute-done | bytes 393248 | tf_op jit(solution)/shard_map/ppermute | solution.py:20
  76.3 4.4 %collective-permute-done.7 = f32[64,3,1,512]{3,0,2,1:T(8,128)S(1)} collective-permute-done((f32[64,3,1,512]{3,0,2,1:T(8,128)S(1)}, f32[64,3,1,512]{3,0,2,1:T(8,128)S(1)}, u32[]{:S(2)}, u32[]{:S(2)}) %collective-permute-start.7) | collective-permute-done | bytes 393248 | tf_op jit(solution)/shard_map/ppermute | solution.py:22
  80.7 3.4 %convert_bitcast_fusion = (bf16[3,8,8,8,512]{4,3,2,1,0:T(8,128)(2,1)S(1)}, f32[64,3,8,512]{3,0,2,1:T(8,128)S(1)}) fusion(f32[64,3,8,512]{3,0,2,1:T(8,128)S(1)} %fusion.25, f32[8]{0:T(128)S(1)} %get-tuple-element.80, f32[8]{0:T(128)S(1)} %get-tuple-element.81, f32[64,3,1,512]{3,0,2,1:T(8,128)S(1)} %collective-permute-done.7, f32[8]{0:T(128)S(1)} %get-tuple-element.79, ...), kind=kLoop, calls=%fused_computation.80 | loop fusion | flops 17301504 | bytes 8650880
  84.7 3.0 %fusion.3 = f32[64,512]{1,0:T(8,128)S(1)} fusion(f32[64,4096]{1,0:T(8,128)S(1)} %bitcast.108, s32[512]{0:T(512)S(1)} %bitcast.117), kind=kOutput, calls=%fused_computation.6 | convolution fusion | flops 1612709888 | bytes 1181696 | tf_op jit(solution)/shard_map/dot_general | solution.py:156
  87.9 4.4 %collective-permute-done.8 = f32[64,512]{1,0:T(8,128)S(1)} collective-permute-done((f32[64,512]{1,0:T(8,128)S(1)}, f32[64,512]{1,0:T(8,128)S(1)}, u32[]{:S(2)}, u32[]{:S(2)}) %collective-permute-start.8) | collective-permute-done | bytes 131104 | tf_op jit(solution)/shard_map/ppermute | solution.py:131
  92.9 3.7 %collective-permute-done.9 = f32[64,512]{1,0:T(8,128)S(1)} collective-permute-done((f32[64,512]{1,0:T(8,128)S(1)}, f32[64,512]{1,0:T(8,128)S(1)}, u32[]{:S(2)}, u32[]{:S(2)}) %collective-permute-start.9) | collective-permute-done | bytes 131104 | tf_op jit(solution)/shard_map/ppermute | solution.py:131
  96.6 4.4 %collective-permute-done.10 = f32[64,512]{1,0:T(8,128)S(1)} collective-permute-done((f32[64,512]{1,0:T(8,128)S(1)}, f32[64,512]{1,0:T(8,128)S(1)}, u32[]{:S(2)}, u32[]{:S(2)}) %collective-permute-start.10) | collective-permute-done | bytes 131104 | tf_op jit(solution)/shard_map/ppermute | solution.py:131
  101.3 1.4 fusion.62
  102.7 1.3 copy.59
  104.1 0.5 fusion.61
  104.6 8.7 %psum.15 = f32[256]{0:T(256)S(1)} all-reduce(f32[256]{0:T(256)S(1)} %bitcast.114), channel_id=1, replica_groups=mesh['groups'=2,'cell'=4,'member'=4] {'cell'}, use_global_device_ids=true, to_apply=%region_9.10 | all-reduce | flops 256 | bytes 2048 | tf_op jit(solution)/shard_map/psum | solution.py:167
  113.3 23.2 %all-reduce.6.cloned.1.call-done = f32[256,256]{1,0:T(8,128)} async-done(((f32[256,256]{1,0:T(8,128)}), f32[256,256]{1,0:T(8,128)}) %all-reduce.6.cloned.1.call-update) | async-done | bytes 262160 | tf_op jit(solution)/shard_map/psum | solution.py:167
  136.4 1.7 select_reduce_fusion
  138.1 1.7 fusion.68
  139.9 35.4 %while.13 = (s32[]{:T(128)}, f32[256,256]{0,1:T(8,128)S(1)}, f32[256,256]{1,0:T(8,128)S(1)}, s32[]{:T(128)}) while((s32[]{:T(128)}, f32[256,256]{0,1:T(8,128)S(1)}, f32[256,256]{1,0:T(8,128)S(1)}, s32[]{:T(128)}) %tuple.51), condition=%wide.region_8.9_spmd.clone, body=%wide.region_7.8_spmd.clone.sunk | while | flops 604241920 | bytes 3407925 | solution.py:82
  140.8 0.6 convolution_bitcast_fusion.3
  142.3 0.6 convolution_bitcast_fusion.3
  143.7 0.6 convolution_bitcast_fusion.3
  145.2 0.6 convolution_bitcast_fusion.3
  146.7 0.6 convolution_bitcast_fusion.3
  148.2 0.6 convolution_bitcast_fusion.3
  149.6 0.6 convolution_bitcast_fusion.3
  151.1 0.6 convolution_bitcast_fusion.3
  152.6 0.6 convolution_bitcast_fusion.3
  154.1 0.6 convolution_bitcast_fusion.3
  155.5 0.6 convolution_bitcast_fusion.3
  157.0 0.6 convolution_bitcast_fusion.3
  158.5 0.6 convolution_bitcast_fusion.3
  159.9 0.6 convolution_bitcast_fusion.3
  161.4 0.6 convolution_bitcast_fusion.3
  162.9 0.6 convolution_bitcast_fusion.3
  164.4 0.6 convolution_bitcast_fusion.3
  165.8 0.6 convolution_bitcast_fusion.3
  167.3 0.6 convolution_bitcast_fusion.3
  168.8 0.6 convolution_bitcast_fusion.3
  170.3 0.6 convolution_bitcast_fusion.3
  171.7 0.6 convolution_bitcast_fusion.3
  173.2 0.6 convolution_bitcast_fusion.3
  174.7 0.6 convolution_bitcast_fusion.3
  176.8 0.8 broadcast_divide_fusion
  177.8 4.0 %fusion.72 = f32[64,3,4096]{2,0,1:T(8,128)S(1)} fusion(bf16[256,3,4096]{2,0,1:T(8,128)(2,1)} %all-gather.2.cloned.1.call-done, f32[256,256]{0,1:T(8,128)S(1)} %get-tuple-element.59, s32[]{:T(128)S(6)} %select_n.37, f32[64]{0:T(128)S(1)} %dynamic-slice), kind=kOutput, calls=%fused_computation.100 | convolution fusion | flops 402702336 | bytes 9503236 | tf_op jit(solution)/shard_map/ij,ifc->jfc/dot_general | solution.py:182
  181.8 2.7 %copy.61 = f32[24,8,8,512]{3,2,1,0:T(8,128)S(1)} copy(f32[24,8,8,512]{3,1,2,0:T(8,128)S(1)} %bitcast.105) | data formatting | bytes 6291456
  184.6 2.0 %copy.58 = f32[64,3,8,512]{3,2,1,0:T(8,128)} copy(f32[64,3,8,512]{3,2,0,1:T(8,128)S(1)} %bitcast.106) | data formatting | bytes 6291456 | tf_op jit(solution)/shard_map/reshape | solution.py:183
  (147 shorter events, 22.8 us)
Async XLA Ops:
  7.4 13.0 %copy-start = (f32[8,2]{0,1:T(2,128)S(1)}, f32[8,2]{0,1:T(2,128)}, u32[]{:S(2)}) copy-start(f32[8,2]{0,1:T(2,128)} %param.10) | copy-start | bytes 196
  7.4 11.5 %copy-start.1 = (s32[8,4]{0,1:T(4,128)S(1)}, s32[8,4]{0,1:T(4,128)}, u32[]{:S(2)}) copy-start(s32[8,4]{0,1:T(4,128)} %param.11) | copy-start | bytes 388
  7.4 129.1 %all-reduce.6.cloned.1.call-start = ((), (), s32[]{:S(2)}) async-start(), calls=%async_computation | async-start | bytes 524288 | tf_op jit(solution)/shard_map/psum | solution.py:167
  11.9 13.6 %collective-permute-start = (f32[64,3,1,512]{3,0,2,1:T(8,128)}, f32[64,3,1,512]{3,0,2,1:T(8,128)}, u32[]{:S(2)}, u32[]{:S(2)}) collective-permute-start(f32[64,3,1,512]{3,0,2,1:T(8,128)} %get-tuple-element.68), channel_id=1, source_target_pairs={{0,4},{4,8},{8,12},{1,5},{5,9},{9,13},{2,6},{6,10},{10,14},{3,7},{... | collective-permute-start | bytes 1179656 | tf_op jit(solution)/shard_map/ppermute | solution.py:20
  17.6 12.6 %collective-permute-start.1 = (f32[64,3,1,512]{3,0,2,1:T(8,128)S(1)}, f32[64,3,1,512]{3,0,2,1:T(8,128)}, u32[]{:S(2)}, u32[]{:S(2)}) collective-permute-start(f32[64,3,1,512]{3,0,2,1:T(8,128)S(1)} %get-tuple-element.69), channel_id=1, source_target_pairs={{4,0},{8,4},{12,8},{5,1},{9,5},{13,9},{6,2},{10,6},{14,10},{7,3},{... | collective-permute-start | bytes 1179656 | tf_op jit(solution)/shard_map/ppermute | solution.py:22
  34.4 9.9 %collective-permute-start.2 = (f32[64,3,1,512]{3,0,2,1:T(8,128)S(1)}, f32[64,3,1,512]{3,0,2,1:T(8,128)S(1)}, u32[]{:S(2)}, u32[]{:S(2)}) collective-permute-start(f32[64,3,1,512]{3,0,2,1:T(8,128)S(1)} %get-tuple-element.66), channel_id=1, source_target_pairs={{0,4},{4,8},{8,12},{1,5},{5,9},{9,13},{2,6},{6,10},{10,14},{3,7},{... | collective-permute-start | bytes 1179656 | tf_op jit(solution)/shard_map/ppermute | solution.py:20
  37.2 11.3 %collective-permute-start.3 = (f32[64,3,1,512]{3,0,2,1:T(8,128)S(1)}, f32[64,3,1,512]{3,0,2,1:T(8,128)S(1)}, u32[]{:S(2)}, u32[]{:S(2)}) collective-permute-start(f32[64,3,1,512]{3,0,2,1:T(8,128)S(1)} %get-tuple-element.67), channel_id=1, source_target_pairs={{4,0},{8,4},{12,8},{5,1},{9,5},{13,9},{6,2},{10,6},{14,10},{7,3},{... | collective-permute-start | bytes 1179656 | tf_op jit(solution)/shard_map/ppermute | solution.py:22
  51.7 9.4 %collective-permute-start.4 = (f32[64,3,1,512]{3,0,2,1:T(8,128)S(1)}, f32[64,3,1,512]{3,0,2,1:T(8,128)S(1)}, u32[]{:S(2)}, u32[]{:S(2)}) collective-permute-start(f32[64,3,1,512]{3,0,2,1:T(8,128)S(1)} %get-tuple-element.64), channel_id=1, source_target_pairs={{0,4},{4,8},{8,12},{1,5},{5,9},{9,13},{2,6},{6,10},{10,14},{3,7},{... | collective-permute-start | bytes 1179656 | tf_op jit(solution)/shard_map/ppermute | solution.py:20
  55.2 10.1 %collective-permute-start.5 = (f32[64,3,1,512]{3,0,2,1:T(8,128)S(1)}, f32[64,3,1,512]{3,0,2,1:T(8,128)S(1)}, u32[]{:S(2)}, u32[]{:S(2)}) collective-permute-start(f32[64,3,1,512]{3,0,2,1:T(8,128)S(1)} %get-tuple-element.65), channel_id=1, source_target_pairs={{4,0},{8,4},{12,8},{5,1},{9,5},{13,9},{6,2},{10,6},{14,10},{7,3},{... | collective-permute-start | bytes 1179656 | tf_op jit(solution)/shard_map/ppermute | solution.py:22
  68.5 7.7 %collective-permute-start.6 = (f32[64,3,1,512]{3,0,2,1:T(8,128)S(1)}, f32[64,3,1,512]{3,0,2,1:T(8,128)S(1)}, u32[]{:S(2)}, u32[]{:S(2)}) collective-permute-start(f32[64,3,1,512]{3,0,2,1:T(8,128)S(1)} %get-tuple-element.62), channel_id=1, source_target_pairs={{0,4},{4,8},{8,12},{1,5},{5,9},{9,13},{2,6},{6,10},{10,14},{3,7},{... | collective-permute-start | bytes 1179656 | tf_op jit(solution)/shard_map/ppermute | solution.py:20
  71.0 9.7 %collective-permute-start.7 = (f32[64,3,1,512]{3,0,2,1:T(8,128)S(1)}, f32[64,3,1,512]{3,0,2,1:T(8,128)S(1)}, u32[]{:S(2)}, u32[]{:S(2)}) collective-permute-start(f32[64,3,1,512]{3,0,2,1:T(8,128)S(1)} %get-tuple-element.63), channel_id=1, source_target_pairs={{4,0},{8,4},{12,8},{5,1},{9,5},{13,9},{6,2},{10,6},{14,10},{7,3},{... | collective-permute-start | bytes 1179656 | tf_op jit(solution)/shard_map/ppermute | solution.py:22
  84.1 0.7 copy-start.4
  84.1 12.6 %copy-start.2 = (f32[1,512]{1,0:T(1,128)S(1)}, f32[1,512]{1,0:T(1,128)}, u32[]{:S(2)}) copy-start(f32[1,512]{1,0:T(1,128)} %param.15) | copy-start | bytes 6148
  84.2 17.0 %copy-start.3 = (f32[1,512]{1,0:T(1,128)S(1)}, f32[1,512]{1,0:T(1,128)}, u32[]{:S(2)}) copy-start(f32[1,512]{1,0:T(1,128)} %param.14) | copy-start | bytes 6148
  87.8 4.4 %collective-permute-start.8 = (f32[64,512]{1,0:T(8,128)S(1)}, f32[64,512]{1,0:T(8,128)S(1)}, u32[]{:S(2)}, u32[]{:S(2)}) collective-permute-start(f32[64,512]{1,0:T(8,128)S(1)} %fusion.3), channel_id=1, source_target_pairs={{0,1},{1,2},{2,3},{3,0},{4,5},{5,6},{6,7},{7,4},{8,9},{9,10},{10,1... | collective-permute-start | bytes 393224 | tf_op jit(solution)/shard_map/ppermute | solution.py:131
  92.2 4.4 %collective-permute-start.9 = (f32[64,512]{1,0:T(8,128)S(1)}, f32[64,512]{1,0:T(8,128)S(1)}, u32[]{:S(2)}, u32[]{:S(2)}) collective-permute-start(f32[64,512]{1,0:T(8,128)S(1)} %collective-permute-done.8), channel_id=1, source_target_pairs={{0,1},{1,2},{2,3},{3,0},{4,5},{5,6},{6,7},{7,4},{8,9},{9,10},{10,1... | collective-permute-start | bytes 393224 | tf_op jit(solution)/shard_map/ppermute | solution.py:131
  96.6 4.4 %collective-permute-start.10 = (f32[64,512]{1,0:T(8,128)S(1)}, f32[64,512]{1,0:T(8,128)S(1)}, u32[]{:S(2)}, u32[]{:S(2)}) collective-permute-start(f32[64,512]{1,0:T(8,128)S(1)} %collective-permute-done.9), channel_id=1, source_target_pairs={{0,1},{1,2},{2,3},{3,0},{4,5},{5,6},{6,7},{7,4},{8,9},{9,10},{10,1... | collective-permute-start | bytes 393224 | tf_op jit(solution)/shard_map/ppermute | solution.py:131
  102.7 75.1 %all-gather.2.cloned.1.call-start = ((), (), s32[]{:S(2)}) async-start(), calls=%async_computation.1 | async-start | bytes 7864320 | tf_op jit(solution)/shard_map/all_gather | solution.py:180
Sparse Core Ops, SparseCore 0:
  102.8 33.6 all-reduce.5
Sparse Core Ops, SparseCore 1:
  104.7 44.5 all-gather.1
